TPU v7x, 512 devices: a whole 4x4x16 slice. The times are simulated.
512 devices in a mesh: blk: 128 (over y_hi, x, z), feat: 4 (over y_lo, core).
Axes of the slice: x: 4, y: 4 (y_hi: 2, y_lo: 2; y = y_hi * 2 + y_lo), z: 16, core: 2. Of those that a mesh axis runs over, the one named last changes fastest.
Arguments:
- points: bfloat16 [16384, 8192], P('blk', 'feat'), may hold values from -12 to 12
- centers: bfloat16 [2048, 8192], P('blk', 'feat'), may hold values from -12 to 12
- coefs: bfloat16 [2048, 1024], P('blk', 'feat'), may hold values from -16 to 16
Outputs:
- normal_prod: float32 [2048, 1024], P('blk', 'feat')
All inputs are finite; a program needn't handle non-finite values.
Results may differ from a plain program's by a relative error of at most 0.0011.
Values may be sent and summed in bfloat16 or wider, within the bound.
A program may use at most 64 MiB of HBM per device.

v0:
```python
import math
import jax
import jax.numpy as jnp
from jax import lax
from jax.sharding import PartitionSpec as P

F = 8192


def on_device(points, centers, coefs):
    point_sq = jnp.einsum("nf,nf->n", points, points, preferred_element_type=jnp.float32)
    center_piece = lax.all_gather(centers, "blk", axis=0, tiled=True)
    center_sq = jnp.einsum(
        "mf,mf->m", center_piece, center_piece, preferred_element_type=jnp.float32
    )
    cross_dot = lax.dot_general(
        points, center_piece, (((1,), (1,)), ((), ())), preferred_element_type=jnp.float32
    )
    dist_tile = point_sq[:, None] + center_sq[None, :] - 2.0 * cross_dot
    all_coefs = lax.all_gather(coefs, "blk", axis=0, tiled=True)
    dist = lax.psum(dist_tile, "feat")
    kernel = jnp.exp(-dist / F).astype(jnp.bfloat16)
    fitted = jnp.dot(kernel, all_coefs, preferred_element_type=jnp.float32).astype(jnp.bfloat16)
    summed = lax.psum_scatter(
        lax.dot_general(
            kernel, fitted, (((0,), (0,)), ((), ())), preferred_element_type=jnp.float32
        ),
        "blk",
        scatter_dimension=0,
        tiled=True,
    )
    point_total = points.shape[0] * lax.axis_size("blk")
    return summed * (1.0 / math.sqrt(point_total))


def solution(mesh):
    in_specs = (P("blk", "feat"), P("blk", "feat"), P("blk", "feat"))
    out_specs = P("blk", "feat")
    return jax.shard_map(
        on_device, mesh=mesh, in_specs=in_specs, out_specs=out_specs, check_vma=False
    )
```

profile of v0, /device:TPU:8, one launch (start us, length us, event | category | flops | bytes accessed | tf_op | source)
XLA Modules:
  0.0 1248.8 jit_solution(10905283807911872829)
XLA Ops:
  6.5 0.0 copy-start.1
  6.5 0.0 all-gather.3.cloned.1.call-start
  6.5 0.7 all-gather.3.cloned.1.call-update
  7.3 0.0 all-gather.5.cloned.1.call-start
  7.3 0.7 all-gather.5.cloned.1.call-update
  8.0 0.0 all-reduce.2.cloned.1.call-start
  8.1 1.2 fusion.3
  9.3 246.9 %all-gather.3.cloned.1.call-done = bf16[2048,2048]{1,0:T(8,128)(2,1)} async-done(((bf16[16,2048]{1,0:T(8,128)(2,1)}), bf16[2048,2048]{1,0:T(8,128)(2,1)}) %all-gather.3.cloned.1.call-update) | async-done | bytes 8388624 | tf_op jit(solution)/shard_map/all_gather | solution.py:12
  256.2 0.0 copy-start
  256.2 5.2 fusion
  261.5 0.0 copy-done.1
  261.5 0.5 copy-done
  262.0 3.9 fusion.1
  265.9 0.0 all-reduce.2.cloned.1.call-update
  265.9 0.0 reduce-scatter.2.cloned.1.call-start
  266.0 184.1 %all-gather.5.cloned.1.call-done = bf16[2048,256]{1,0:T(8,128)(2,1)} async-done(((bf16[16,256]{1,0:T(8,128)(2,1)}), bf16[2048,256]{1,0:T(8,128)(2,1)}) %all-gather.5.cloned.1.call-update) | async-done | bytes 1048592 | tf_op jit(solution)/shard_map/all_gather | solution.py:20
  450.1 54.6 %all-reduce.2.cloned.1.call-done = f32[128,2048]{1,0:T(8,128)} async-done(((f32[128,2048]{1,0:T(8,128)}), f32[128,2048]{1,0:T(8,128)}) %all-reduce.2.cloned.1.call-update) | async-done | bytes 1048592 | tf_op jit(solution)/shard_map/psum | solution.py:21
  504.7 4.2 fusion.2
  508.9 0.0 reduce-scatter.2.cloned.1.call-update
  508.9 732.0 %reduce-scatter.2.cloned.1.call-done = f32[16,256]{1,0:T(8,128)} async-done(((f32[2048,256]{1,0:T(8,128)}), f32[16,256]{1,0:T(8,128)}) %reduce-scatter.2.cloned.1.call-update) | async-done | bytes 16400 | tf_op jit(solution)/shard_map/reduce_scatter | solution.py:24
  1241.0 1.3 broadcast_multiply_fusion
Async XLA Ops:
  6.5 254.9 %copy-start.1 = (bf16[128,2048]{1,0:T(8,128)(2,1)S(1)}, bf16[128,2048]{1,0:T(8,128)(2,1)}, u32[]{:S(2)}) copy-start(bf16[128,2048]{1,0:T(8,128)(2,1)} %param.3) | copy-start | bytes 1572868
  6.5 249.7 %all-gather.3.cloned.1.call-start = ((), (), s32[]{:S(2)}) async-start(), calls=%async_computation.1 | async-start | bytes 8454144 | tf_op jit(solution)/shard_map/all_gather | solution.py:12
  7.3 442.8 %all-gather.5.cloned.1.call-start = ((), (), s32[]{:S(2)}) async-start(), calls=%async_computation.3 | async-start | bytes 1056768 | tf_op jit(solution)/shard_map/all_gather | solution.py:20
  8.0 496.7 %all-reduce.2.cloned.1.call-start = ((), (), s32[]{:S(2)}) async-start(), calls=%async_computation.2 | async-start | bytes 2097152 | tf_op jit(solution)/shard_map/psum | solution.py:21
  256.2 5.8 copy-start
  265.9 975.0 %reduce-scatter.2.cloned.1.call-start = ((), (), s32[]{:S(2)}) async-start(), calls=%async_computation.4 | async-start | bytes 2113536 | tf_op jit(solution)/shard_map/reduce_scatter | solution.py:24
Sparse Core Ops, SparseCore 0:
  11.8 244.3 all-gather.2
  260.5 189.5 all-gather.4
  453.1 51.5 all-reduce.1
  509.0 731.8 reduce-scatter.1
where the time goes:
time: 1250 us
  waiting for transfers between devices  1220 us (98%)
  between operations  13.1 us (1%)
    reduce_scatter x1, waiting for transfers between devices, on_device(): lax.psum_scatter(lax.dot_general(kernel, fitted, (((0,), (0,)), ((), ()))...  732 us
    all_gather x1, waiting for transfers between devices, on_device(): center_piece = lax.all_gather(centers, 'blk', axis=0, tiled=True)  247 us
    all_gather x1, waiting for transfers between devices, on_device(): all_coefs = lax.all_gather(coefs, 'blk', axis=0, tiled=True)  184 us
    psum x1, waiting for transfers between devices, on_device(): dist = lax.psum(dist_tile, 'feat')  54.6 us
  transfers between devices with their start and end apart: 4, of which 4 were waited for; matrix products, arithmetic and copies ran while one was open for 1% of the time, Pallas kernels for 0%

commit v1 on v0

--- a/solution.py
+++ b/solution.py
@@ -3,6 +3,7 @@
 import jax.numpy as jnp
 from jax import lax
 from jax.sharding import PartitionSpec as P
+from jax.lax import all_to_all, psum
 
 F = 8192
 
@@ -17,7 +18,10 @@
         points, center_piece, (((1,), (1,)), ((), ())), preferred_element_type=jnp.float32
     )
     dist_tile = point_sq[:, None] + center_sq[None, :] - 2.0 * cross_dot
-    all_coefs = lax.all_gather(coefs, "blk", axis=0, tiled=True)
+    so_far_all = []
+    for _ in range(psum(1, "blk")):
+        so_far_all.append(coefs)
+    all_coefs = jnp.concatenate(all_to_all(jnp.stack(so_far_all), "blk", 0, 0), axis=0)
     dist = lax.psum(dist_tile, "feat")
     kernel = jnp.exp(-dist / F).astype(jnp.bfloat16)
     fitted = jnp.dot(kernel, all_coefs, preferred_element_type=jnp.float32).astype(jnp.bfloat16)

time: 1250 us -> 1070 us (0.86)
  waiting for transfers between devices: 1220 us -> 1010 us
  starting transfers between devices: 0.12 us -> 21.6 us
    all_gather x1 -> x0, waiting for transfers between devices: 184 us -> none  [on_device(): all_coefs = lax.all_gather(coefs, 'blk', axis=0, tiled=True)]
    all_to_all x0 -> x1, starting transfers between devices: none -> 21.5 us  [on_device(): all_to_all(jnp.stack(so_far_all), 'blk', 0, 0)]
    all_gather x1, waiting for transfers between devices: 247 us -> 228 us  [on_device(): center_piece = lax.all_gather(centers, 'blk', axis=0, tiled=True)]
  transfers between devices with their start and end apart: 4 -> 4, of which waited for: 4 -> 3; matrix products, arithmetic and copies ran while one was open for 1% -> 1% of each run, Pallas kernels for 0% -> 0%
where the time goes in v1:
time: 1070 us
  waiting for transfers between devices  1010 us (94%)
  starting transfers between devices  21.6 us (2%)
  between operations  13.1 us (1%)
    reduce_scatter x1, waiting for transfers between devices, on_device(): lax.psum_scatter(lax.dot_general(kernel, fitted, (((0,), (0,)), ((), ()))...  732 us
    all_gather x1, waiting for transfers between devices, on_device(): center_piece = lax.all_gather(centers, 'blk', axis=0, tiled=True)  228 us
    psum x1, waiting for transfers between devices, on_device(): dist = lax.psum(dist_tile, 'feat')  51.8 us
    all_to_all x1, starting transfers between devices, on_device(): all_to_all(jnp.stack(so_far_all), 'blk', 0, 0)  21.5 us
  transfers between devices with their start and end apart: 4, of which 3 were waited for; matrix products, arithmetic and copies ran while one was open for 1% of the time, Pallas kernels for 0%

profile of v1, /device:TPU:8, one launch (start us, length us, event | category | flops | bytes accessed | tf_op | source)
XLA Modules:
  0.0 1065.2 jit_solution(4306252619298720124)
XLA Ops:
  6.5 0.0 copy-start.1
  6.5 0.0 all-gather.2.cloned.1.call-start
  6.5 0.7 all-gather.2.cloned.1.call-update
  7.3 1.8 stack.2
  9.1 21.5 %all-to-all-start = ((bf16[128,16,256]{2,1,0:T(8,128)(2,1)}), bf16[128,16,256]{2,1,0:T(8,128)(2,1)S(1)}, u32[]{:S(2)}, u32[]{:S(2)}) async-start(bf16[128,16,256]{2,1,0:T(8,128)(2,1)} %stack.2), calls=%async_computation | async-start | bytes 2097152 | tf_op jit(solution)/shard_map/all_to_all | solution.py:24
  30.6 0.0 all-reduce.2.cloned.1.call-start
  30.6 1.2 fusion.3
  31.9 227.9 %all-gather.2.cloned.1.call-done = bf16[2048,2048]{1,0:T(8,128)(2,1)} async-done(((bf16[16,2048]{1,0:T(8,128)(2,1)}), bf16[2048,2048]{1,0:T(8,128)(2,1)}) %all-gather.2.cloned.1.call-update) | async-done | bytes 8388624 | tf_op jit(solution)/shard_map/all_gather | solution.py:13
  259.8 0.0 copy-start
  259.8 5.2 fusion
  265.0 0.0 copy-done.1
  265.0 0.5 copy-done
  265.5 3.9 fusion.1
  269.4 0.0 all-reduce.2.cloned.1.call-update
  269.5 0.0 reduce-scatter.2.cloned.1.call-start
  269.5 0.0 all-to-all-done
  269.5 51.8 %all-reduce.2.cloned.1.call-done = f32[128,2048]{1,0:T(8,128)} async-done(((f32[128,2048]{1,0:T(8,128)}), f32[128,2048]{1,0:T(8,128)}) %all-reduce.2.cloned.1.call-update) | async-done | bytes 1048592 | tf_op jit(solution)/shard_map/psum | solution.py:25
  321.3 3.9 fusion.2
  325.3 0.0 reduce-scatter.2.cloned.1.call-update
  325.3 732.0 %reduce-scatter.2.cloned.1.call-done = f32[16,256]{1,0:T(8,128)} async-done(((f32[2048,256]{1,0:T(8,128)}), f32[16,256]{1,0:T(8,128)}) %reduce-scatter.2.cloned.1.call-update) | async-done | bytes 16400 | tf_op jit(solution)/shard_map/reduce_scatter | solution.py:28
  1057.3 1.3 broadcast_multiply_fusion
Async XLA Ops:
  6.5 258.5 %copy-start.1 = (bf16[128,2048]{1,0:T(8,128)(2,1)S(1)}, bf16[128,2048]{1,0:T(8,128)(2,1)}, u32[]{:S(2)}) copy-start(bf16[128,2048]{1,0:T(8,128)(2,1)} %param.3) | copy-start | bytes 1572868
  6.5 253.2 %all-gather.2.cloned.1.call-start = ((), (), s32[]{:S(2)}) async-start(), calls=%async_computation.2 | async-start | bytes 8454144 | tf_op jit(solution)/shard_map/all_gather | solution.py:13
  9.1 260.4 %all-to-all-start = ((bf16[128,16,256]{2,1,0:T(8,128)(2,1)}), bf16[128,16,256]{2,1,0:T(8,128)(2,1)S(1)}, u32[]{:S(2)}, u32[]{:S(2)}) async-start(bf16[128,16,256]{2,1,0:T(8,128)(2,1)} %stack.2), calls=%async_computation | async-start | bytes 2097152 | tf_op jit(solution)/shard_map/all_to_all | solution.py:24
  30.6 290.8 %all-reduce.2.cloned.1.call-start = ((), (), s32[]{:S(2)}) async-start(), calls=%async_computation.3 | async-start | bytes 2097152 | tf_op jit(solution)/shard_map/psum | solution.py:25
  259.8 5.8 copy-start
  269.5 787.8 %reduce-scatter.2.cloned.1.call-start = ((), (), s32[]{:S(2)}) async-start(), calls=%async_computation.4 | async-start | bytes 2113536 | tf_op jit(solution)/shard_map/reduce_scatter | solution.py:28
Sparse Core Ops, SparseCore 0:
  11.8 247.8 all-gather.1
  269.6 51.7 all-reduce.1
  325.4 731.8 reduce-scatter.1
